TPU v7x, 32 devices: a whole 2x2x4 slice. The times are simulated.
32 devices in a mesh: wave: 4 (over z), tile: 8 (over y, x, core).
Axes of the slice: x: 2, y: 2, z: 4, core: 2. Of those that a mesh axis runs over, the one named last changes fastest.
Arguments:
- spectral: bfloat16 [640, 2, 64, 1281], P('wave', None, 'tile'), may hold values from -0.083496094 to 0.083496094
- legendre: bfloat16 [640, 8, 1281], P('wave'), may hold values from -0.25 to 0.25
- pair_ids: int32 [640], replicated, may hold values from 0 to 639, each once
Outputs:
- spectral_out: bfloat16 [640, 2, 64, 1281], P('wave', None, 'tile')
Inputs may be any that keep to these rules, and one draw needn't show every extreme that they name: A permutation: each pair 0 to 639 appears once; slot s of spectral, legendre and spectral_out holds wavenumbers pair_ids[s] and 1279 - pair_ids[s].
All inputs are finite; a program needn't handle non-finite values.
Results may differ from a plain program's by a relative error of at most 0.0072.
Values may be sent and summed in bfloat16 or wider, within the bound.
A program may use at most 64 MiB of HBM per device.

v0:
```python
import functools
import math
import jax
import jax.numpy as jnp
from jax import lax
from jax.sharding import PartitionSpec as P

MW = 1280
HALF_LATS = 1280
PAIRS = 640
NPTS = 5156
LANES = 128
RADIX = 32
F32 = jnp.float32
BF16 = jnp.bfloat16


def cycle_lengths(pair_number, pair_total):
    polar_cycle = pair_number * (HALF_LATS // 2) // pair_total
    cycle_index = jnp.stack([polar_cycle, HALF_LATS - 1 - polar_cycle])
    return (cycle_index, 20 + 4 * cycle_index)


def cycle_scale(cycle_index, cycle_len, lat_count):
    angles = math.pi * (cycle_index.astype(F32) + 0.5) / (2.0 * HALF_LATS)
    return 40.0 * jnp.sin(angles) / jnp.sqrt(lat_count * cycle_len.astype(F32))


def trig(wavenumbers, local_index, length):
    phase = wavenumbers[:, None] * local_index[None, :] % length[None, :]
    angles = 2.0 * math.pi * phase.astype(F32) / length[None, :].astype(F32)
    return (jnp.cos(angles), jnp.sin(angles))


def tables(local_index, length):
    outer = MW // 2 // RADIX
    a_cos, a_sin = trig(2 * RADIX * lax.iota(jnp.int32, outer), local_index, length)
    b_cos, b_sin = trig(lax.iota(jnp.int32, 2 * RADIX), local_index, length)
    pts = local_index.shape[0]
    b_cos = b_cos.reshape(RADIX, 2, pts).transpose(1, 0, 2)[:, None]
    b_sin = b_sin.reshape(RADIX, 2, pts).transpose(1, 0, 2)[:, None]
    a_cos, a_sin = (a_cos[None, :, None], a_sin[None, :, None])
    cos = (a_cos * b_cos - a_sin * b_sin).astype(BF16).reshape(2, MW // 2, pts)
    sin = (a_sin * b_cos + a_cos * b_sin).astype(BF16).reshape(2, MW // 2, pts)
    return (cos, sin)


def grid_products(grid_values):
    layer_count = grid_values.shape[0] // 4
    u, w, t, q = grid_values.astype(F32).reshape(4, layer_count, grid_values.shape[1])
    level = lax.iota(jnp.int32, layer_count)
    acc, rows = (t[layer_count - 1], [])
    rows.append(acc)
    for v in range(layer_count - 2, -1, -1):
        acc = acc + t[v]
        rows.append(acc)
    geo = jnp.stack(rows[::-1]) / math.sqrt(layer_count)
    energy = 0.5 * (u * u + w * w) + geo
    return jnp.stack([energy, u * t, w * t, u * q]).reshape(grid_values.shape).astype(BF16)


def local(spectral, legendre, pair_ids):
    slots, _, cols, row_total = spectral.shape
    lat_count = legendre.shape[1]
    tiles = lax.axis_size("tile")
    zero = jnp.zeros((), BF16)
    wave_here = lax.axis_index("wave")
    slot_ids = lax.dynamic_slice_in_dim(pair_ids, wave_here * slots, slots)
    row_index = lax.broadcasted_iota(jnp.int32, (slots, row_total), 1)
    upper = (row_index >= (MW - slot_ids)[:, None])[:, None, :]
    masked = jnp.concatenate(
        [jnp.where(upper, zero, legendre), jnp.where(upper, legendre, zero)], axis=1
    )
    spec = spectral.reshape(slots, 2 * cols, row_total)
    cycle_index, cycle_len = cycle_lengths(wave_here, lat_count // 2)
    scales = cycle_scale(cycle_index, cycle_len, lat_count)
    quarter = NPTS // 4
    step = (
        tiles * LANES // math.gcd(4, tiles) if tiles * LANES // math.gcd(4, tiles) <= 512 else 512
    )
    kpad = -(-quarter // step) * step
    k = lax.iota(jnp.int32, kpad)
    q0 = cycle_len[0] // 4
    second = k >= q0
    inside = k < quarter
    local_index = jnp.where(inside, k - jnp.where(second, q0, 0), 0)
    length = jnp.where(second, cycle_len[1], cycle_len[0])
    cos, sin = tables(local_index, length)
    half = MW // 2
    m_order = jnp.arange(MW, dtype=jnp.int32).reshape(half, 2).T
    quarter_m = half // 2
    m0, m1 = (m_order[:, :quarter_m], m_order[:, quarter_m:])
    q_of = jnp.stack([m0, MW - 1 - m1]).reshape(2, half)
    hot = (pair_ids[None, :, None] == q_of[:, None, :]).astype(BF16)
    coefficients = (
        lax.dot_general(masked, spec, (((2,), (2,)), ((0,), (0,))), preferred_element_type=F32)
        .astype(BF16)
        .reshape(slots, 2, lat_count, 2 * cols)
    )
    coefficients = coefficients.transpose(2, 1, 3, 0)
    fourier = lax.all_to_all(coefficients, "wave", split_axis=0, concat_axis=3, tiled=True)
    ordered = lax.dot_general(
        fourier, hot, (((3,), (1,)), ((1,), (0,))), preferred_element_type=F32
    )
    ordered = ordered.reshape(2, 2, 2, cols, 2, quarter_m).transpose(4, 2, 1, 3, 0, 5)
    ordered = ordered.reshape(2, 2, 2, cols, half)
    factor = jnp.where(m_order == 0, 1.0, 2.0).astype(F32)
    keep = 2 * m_order[:, None, :] < cycle_len[None, :, None]
    ordered = ordered * jnp.where(keep, factor[:, None, :], 0.0)[:, None, :, None, :]
    sign = jnp.where(m_order // 2 % 2 == 0, 1.0, -1.0).astype(F32)
    re, im = (ordered[:, 0].reshape(2, 2 * cols, half), ordered[:, 1].reshape(2, 2 * cols, half))
    even_c = jnp.concatenate([re[0], re[0] * sign[0]]).astype(BF16)
    even_s = jnp.concatenate([-im[0], -im[0] * sign[0]]).astype(BF16)
    odd_c = jnp.concatenate([re[1], im[1] * sign[1]]).astype(BF16)
    odd_s = jnp.concatenate([-im[1], re[1] * sign[1]]).astype(BF16)
    dot = functools.partial(jnp.dot, preferred_element_type=F32)
    even = (dot(even_c, cos[0]) + dot(even_s, sin[0])).reshape(2, 2, cols, kpad)
    odd = (dot(odd_c, cos[1]) + dot(odd_s, sin[1])).reshape(2, 2, cols, kpad)
    even = jnp.where(second, even[:, 1], even[:, 0])
    odd = jnp.where(second, odd[:, 1], odd[:, 0])
    grid_values = jnp.stack(
        [even[0] + odd[0], even[1] - odd[1], even[0] - odd[0], even[1] + odd[1]], axis=1
    ).astype(BF16)
    grid_values = grid_values.reshape(cols, 4 * kpad)
    grid_values = lax.all_to_all(grid_values, "tile", split_axis=1, concat_axis=0, tiled=True)
    product = grid_products(grid_values)
    product = lax.all_to_all(product, "tile", split_axis=0, concat_axis=1, tiled=True)
    x = product.astype(F32).reshape(cols, 4, kpad)
    x = jnp.where(inside, x, 0.0)
    x0, x1, x2, x3 = (x[:, 0], x[:, 1], x[:, 2], x[:, 3])

    def by_lat(a, b):
        both = jnp.stack([a, b])[:, None]
        return (
            jnp.where(second == (lax.iota(jnp.int32, 2) == 1)[None, :, None, None], both, 0.0)
            .astype(BF16)
            .reshape(4 * cols, kpad)
        )

    even_in = by_lat(x0 + x2 + (x1 + x3), x0 + x2 - (x1 + x3))
    odd_in = by_lat(x0 - x2, x1 - x3)
    nt = lambda a, b: lax.dot_general(
        a, b, (((1,), (1,)), ((), ())), preferred_element_type=F32
    ).reshape(2, 2, cols, half)
    ec, es = (nt(even_in, cos[0]), nt(even_in, sin[0]))
    oc, os_ = (nt(odd_in, cos[1]), nt(odd_in, sin[1]))
    pick = sign[0] > 0
    even_re = jnp.where(pick, ec[0], ec[1])
    even_im = -jnp.where(pick, es[0], es[1])
    odd_re = oc[0] - sign[1] * os_[1]
    odd_im = -os_[0] - sign[1] * oc[1]
    back = jnp.stack([jnp.stack([even_re, even_im]), jnp.stack([odd_re, odd_im])])
    back = back * jnp.where(keep, scales[None, :, None], 0.0)[:, None, :, None, :]
    back = back.astype(BF16).reshape(2, 2, 2, cols, 2, quarter_m).transpose(4, 2, 1, 3, 0, 5)
    back = back.reshape(2, 4 * cols, half)
    back = lax.dot_general(
        back, hot, (((2,), (2,)), ((0,), (0,))), preferred_element_type=F32
    ).astype(BF16)
    back = back.reshape(2, 2, 2 * cols, PAIRS).transpose(1, 0, 2, 3)
    returned = lax.all_to_all(back, "wave", split_axis=3, concat_axis=0, tiled=True)
    returned = returned.transpose(3, 2, 1, 0).reshape(slots, 2 * cols, 2 * lat_count)
    result = lax.dot_general(
        returned, masked, (((2,), (1,)), ((0,), (0,))), preferred_element_type=F32
    )
    return result.reshape(slots, 2, cols, row_total).astype(BF16)


def solution(mesh):
    placed = (P("wave", None, "tile", None), P("wave", None, None), P())
    return jax.shard_map(
        local, mesh=mesh, in_specs=placed, out_specs=P("wave", None, "tile", None), check_vma=False
    )
```

profile of v0, /device:TPU:0, one launch (start us, length us, event | category | flops | bytes accessed | tf_op | source)
XLA Modules:
  0.0 97.7 jit_solution(9886017591165895922)
XLA Ops:
  0.0 0.8 dynamic-slice_subtract_fusion
  1.0 5.1 %broadcast_select_fusion.1 = (bf16[160,8,1281]{2,1,0:T(8,128)(2,1)}, bf16[160,8,1281]{2,1,0:T(8,128)(2,1)}) fusion(bf16[160,8,1281]{2,1,0:T(8,128)(2,1)} %param.4, pred[160,1281]{1,0:T(8,128)(4,1)S(1)} %iota_compare_fusion), kind=kLoop, calls=%fused_computation.10 | loop fusion | flops 3279360 | bytes 10043040 | tf_op jit(solution)/shard_map/jit(_where)/select_n | solution.py:72
  6.1 8.6 %fusion.12 = bf16[160,2,8,16]{3,2,1,0:T(8,128)(2,1)S(1)} fusion(bf16[160,2,8,1281]{3,2,1,0:T(8,128)(2,1)} %param.3, bf16[160,8,1281]{2,1,0:T(8,128)(2,1)} %get-tuple-element.27, bf16[160,8,1281]{2,1,0:T(8,128)(2,1)} %get-tuple-element.26), kind=kOutput, calls=%fused_computation.19 | convolution fusion | flops 118097920 | bytes 13199360 | tf_op jit(solution)/shard_map/dot_general | solution.py:96
  14.6 1.2 %copy.44 = bf16[160,2,8,16]{0,3,1,2:T(8,128)(2,1)} copy(bf16[160,2,8,16]{3,2,1,0:T(8,128)(2,1)S(1)} %fusion.12) | data formatting | bytes 163840 | tf_op jit(solution)/shard_map/reshape | solution.py:98
  15.9 6.3 %all-to-all-start = ((bf16[8,2,16,160]{3,2,1,0:T(8,128)(2,1)}), bf16[8,2,16,160]{3,2,1,0:T(8,128)(2,1)S(1)}, u32[]{:S(2)}, u32[]{:S(2)}) async-start(bf16[8,2,16,160]{3,2,1,0:T(8,128)(2,1)} %bitcast.5), calls=%async_computation | async-start | bytes 262144 | tf_op jit(solution)/shard_map/all_to_all | solution.py:101
  25.6 1.3 %iota_compare_fusion.2 = (pred[1536]{0:T(1024)(128)(4,1)S(1)}, pred[1536]{0:T(1024)(128)(4,1)S(1)}) fusion(s32[]{:T(128)S(6)} %select_n.232, s32[]{:T(128)} %bitcast.2, s32[]{:T(128)} %bitcast.13), kind=kLoop, calls=%fused_computation.136 | loop fusion | flops 7680 | bytes 3084 | tf_op jit(solution)/shard_map/ge | solution.py:84
  26.9 1.3 %compare_select_fusion.1 = (s32[1536]{0:T(1024)S(1)}, f32[1536]{0:T(1024)S(1)}) fusion(s32[]{:T(128)} %bitcast.2, s32[]{:T(128)} %bitcast.13, s32[]{:T(128)S(6)} %select_n.232), kind=kLoop, calls=%fused_computation.123 | loop fusion | flops 7680 | bytes 12300 | tf_op jit(solution)/shard_map/jit(remainder)/jit(_where)/select_n | solution.py:30
  28.3 2.1 %fusion.39 = (f32[20,1536]{1,0:T(8,128)S(1)}, f32[20,1536]{1,0:T(8,128)S(1)}) fusion(f32[1536]{0:T(1024)S(1)} %get-tuple-element.78, pred[1536]{0:T(1024)(128)(4,1)S(1)} %get-tuple-element.80, s32[1536]{0:T(1024)S(1)} %get-tuple-element.77, s32[1536]{0:T(1024)S(1)} %subtract_select_fusion, s32[20]{0:T(128)S(1)} %iota_multiply_fusion), kind=kLoop, calls=%fused_computation.65 | loop fusion | flops 337920 | bytes 265808 | tf_op jit(solution)/shard_map/cos | solution.py:32
  30.3 5.3 %fusion.27 = (f32[2,32,1536]{2,1,0:T(8,128)S(1)}, f32[2,32,1536]{2,1,0:T(8,128)S(1)}) fusion(f32[1536]{0:T(1024)S(1)} %get-tuple-element.78, pred[1536]{0:T(1024)(128)(4,1)S(1)} %get-tuple-element.80, s32[1536]{0:T(1024)S(1)} %get-tuple-element.77, s32[1536]{0:T(1024)S(1)} %subtract_select_fusion, s32[2,32]{1,0:T(2,128)S(1)} %multiply_add_fusion.1), kind=kLoop, calls=%fused_computation.40 | loop fusion | flops 1081344 | bytes 806656 | tf_op jit(solution)/shard_map/cos | solution.py:32
  35.6 2.5 %add_convert_fusion = (bf16[2,20,32,1536]{3,2,1,0:T(8,128)(2,1)S(1)}, bf16[2,20,32,1536]{3,2,1,0:T(8,128)(2,1)S(1)}) fusion(f32[2,32,1536]{2,1,0:T(8,128)S(1)} %get-tuple-element.62, f32[20,1536]{1,0:T(8,128)S(1)} %get-tuple-element.64, f32[2,32,1536]{2,1,0:T(8,128)S(1)} %get-tuple-element.61, f32[20,1536]{1,0:T(8,128)S(1)} %get-tuple-element.63), kind=kLoop, calls=%fused_computation | loop fusion | flops 15728640 | bytes 8896512 | tf_op jit(solution)/shard_map/convert_element_type | solution.py:44
  38.1 1.5 %fusion.75 = (bf16[1,20,32,1536]{3,2,1,0:T(8,128)(2,1)}, bf16[1,20,32,1536]{3,2,1,0:T(8,128)(2,1)S(1)}) fusion(bf16[2,20,32,1536]{3,2,1,0:T(8,128)(2,1)S(1)} %get-tuple-element.28), kind=kLoop, calls=%fused_computation.178 | loop fusion | bytes 7864320 | tf_op jit(solution)/shard_map/slice | solution.py:117
  39.6 2.3 %fusion.76 = (bf16[1,20,32,1536]{3,2,1,0:T(8,128)(2,1)}, bf16[1,20,32,1536]{3,2,1,0:T(8,128)(2,1)}) fusion(bf16[2,20,32,1536]{3,2,1,0:T(8,128)(2,1)S(1)} %get-tuple-element.29), kind=kLoop, calls=%fused_computation.179 | loop fusion | bytes 7864320 | tf_op jit(solution)/shard_map/slice | solution.py:117
  42.7 0.7 fusion.4
  44.0 2.1 %fusion.43 = f32[32,1536]{1,0:T(8,128)S(1)} fusion(bf16[640,1536]{1,0:T(8,128)(2,1)} %bitcast.174, bf16[16,640]{1,0:T(8,128)(2,1)S(1)} %get-tuple-element.43, bf16[16,640]{1,0:T(8,128)(2,1)S(1)} %get-tuple-element.49), kind=kOutput, calls=%fused_computation.92 | convolution fusion | flops 62996480 | bytes 2203648 | tf_op jit(solution)/shard_map/dot_general | solution.py:117
  46.1 2.0 %fusion.50 = f32[32,1536]{1,0:T(8,128)S(1)} fusion(bf16[640,1536]{1,0:T(8,128)(2,1)} %bitcast.170, bf16[16,640]{1,0:T(8,128)(2,1)S(1)} %get-tuple-element.47, bf16[16,640]{1,0:T(8,128)(2,1)S(1)} %get-tuple-element.50), kind=kOutput, calls=%fused_computation.99 | convolution fusion | flops 62996480 | bytes 2203648 | tf_op jit(solution)/shard_map/dot_general | solution.py:118
  49.8 3.7 %all-to-all-start.1 = ((bf16[8,8,768]{2,0,1:T(8,128)(2,1)}), bf16[8,8,768]{2,0,1:T(8,128)(2,1)S(1)}, u32[]{:S(2)}, u32[]{:S(2)}) async-start(bf16[8,8,768]{2,0,1:T(8,128)(2,1)} %bitcast.31), calls=%async_computation.1 | async-start | bytes 196608 | tf_op jit(solution)/shard_map/all_to_all | solution.py:125
  53.6 5.1 %all-to-all-done.1 = bf16[8,8,768]{2,0,1:T(8,128)(2,1)S(1)} async-done(((bf16[8,8,768]{2,0,1:T(8,128)(2,1)}), bf16[8,8,768]{2,0,1:T(8,128)(2,1)S(1)}, u32[]{:S(2)}, u32[]{:S(2)}) %all-to-all-start.1) | async-done | bytes 98336 | tf_op jit(solution)/shard_map/all_to_all | solution.py:125
  59.6 3.4 %all-to-all-start.2 = ((bf16[8,8,768]{2,1,0:T(8,128)(2,1)}), bf16[8,8,768]{2,1,0:T(8,128)(2,1)S(1)}, u32[]{:S(2)}, u32[]{:S(2)}) async-start(bf16[8,8,768]{2,1,0:T(8,128)(2,1)} %bitcast.40), calls=%async_computation.2 | async-start | bytes 196608 | tf_op jit(solution)/shard_map/all_to_all | solution.py:127
  62.9 5.1 %all-to-all-done.2 = bf16[8,8,768]{2,1,0:T(8,128)(2,1)S(1)} async-done(((bf16[8,8,768]{2,1,0:T(8,128)(2,1)}), bf16[8,8,768]{2,1,0:T(8,128)(2,1)S(1)}, u32[]{:S(2)}, u32[]{:S(2)}) %all-to-all-start.2) | async-done | bytes 98336 | tf_op jit(solution)/shard_map/all_to_all | solution.py:127
  68.2 2.3 %fusion.84 = f32[32,640]{1,0:T(8,128)S(1)} fusion(bf16[32,1536]{1,0:T(8,128)(2,1)S(1)} %bitcast.179, bf16[640,1536]{1,0:T(8,128)(2,1)} %bitcast.172), kind=kOutput, calls=%fused_computation.188 | convolution fusion | flops 62914560 | bytes 2146304 | tf_op jit(solution)/shard_map/dot_general | solution.py:142
  74.7 0.9 copy.54
  76.7 10.7 %all_to_all.56 = bf16[4,2,5120]{2,1,0:T(2,128)(2,1)S(1)} all-to-all(bf16[4,2,5120]{2,1,0:T(2,128)(2,1)S(1)} %reshape.950), channel_id=1, replica_groups=mesh['wave'=4,'tile'=8] {'wave'}, dimensions={0} | all-to-all | bytes 163840 | tf_op jit(solution)/shard_map/all_to_all | solution.py:160
  87.8 0.9 copy.60
  89.4 8.3 %convert_bitcast_fusion = bf16[160,2,8,1281]{3,2,1,0:T(8,128)(2,1)} fusion(bf16[160,16,16]{2,1,0:T(8,128)(2,1)S(1)} %copy.58, bf16[160,8,1281]{2,1,0:T(8,128)(2,1)} %get-tuple-element.27, bf16[160,8,1281]{2,1,0:T(8,128)(2,1)} %get-tuple-element.26), kind=kOutput, calls=%fused_computation.5 | convolution fusion | flops 121336320 | bytes 13199360 | tf_op jit(solution)/shard_map/dot_general | solution.py:162
  (89 shorter events, 11.4 us)
Async XLA Ops:
  15.9 26.6 %all-to-all-start = ((bf16[8,2,16,160]{3,2,1,0:T(8,128)(2,1)}), bf16[8,2,16,160]{3,2,1,0:T(8,128)(2,1)S(1)}, u32[]{:S(2)}, u32[]{:S(2)}) async-start(bf16[8,2,16,160]{3,2,1,0:T(8,128)(2,1)} %bitcast.5), calls=%async_computation | async-start | bytes 262144 | tf_op jit(solution)/shard_map/all_to_all | solution.py:101
  39.6 3.0 %copy-start.3 = (s32[640]{0:T(1024)S(1)}, s32[640]{0:T(1024)}, u32[]{:S(2)}) copy-start(s32[640]{0:T(1024)} %param.5) | copy-start | bytes 7684
  43.9 4.2 %copy-start.1 = (bf16[1,20,32,1536]{3,2,1,0:T(8,128)(2,1)S(1)}, bf16[1,20,32,1536]{3,2,1,0:T(8,128)(2,1)}, u32[]{:S(2)}) copy-start(bf16[1,20,32,1536]{3,2,1,0:T(8,128)(2,1)} %get-tuple-element.22) | copy-start | bytes 5898244
  49.8 8.9 %all-to-all-start.1 = ((bf16[8,8,768]{2,0,1:T(8,128)(2,1)}), bf16[8,8,768]{2,0,1:T(8,128)(2,1)S(1)}, u32[]{:S(2)}, u32[]{:S(2)}) async-start(bf16[8,8,768]{2,0,1:T(8,128)(2,1)} %bitcast.31), calls=%async_computation.1 | async-start | bytes 196608 | tf_op jit(solution)/shard_map/all_to_all | solution.py:125
  59.6 8.5 %all-to-all-start.2 = ((bf16[8,8,768]{2,1,0:T(8,128)(2,1)}), bf16[8,8,768]{2,1,0:T(8,128)(2,1)S(1)}, u32[]{:S(2)}, u32[]{:S(2)}) async-start(bf16[8,8,768]{2,1,0:T(8,128)(2,1)} %bitcast.40), calls=%async_computation.2 | async-start | bytes 196608 | tf_op jit(solution)/shard_map/all_to_all | solution.py:127
  68.0 2.5 %copy-start.2 = (bf16[1,20,32,1536]{3,2,1,0:T(8,128)(2,1)S(1)}, bf16[1,20,32,1536]{3,2,1,0:T(8,128)(2,1)}, u32[]{:S(2)}) copy-start(bf16[1,20,32,1536]{3,2,1,0:T(8,128)(2,1)} %get-tuple-element.24) | copy-start | bytes 5898244
  68.1 3.8 %copy-start = (bf16[1,20,32,1536]{3,2,1,0:T(8,128)(2,1)S(1)}, bf16[1,20,32,1536]{3,2,1,0:T(8,128)(2,1)}, u32[]{:S(2)}) copy-start(bf16[1,20,32,1536]{3,2,1,0:T(8,128)(2,1)} %get-tuple-element.25) | copy-start | bytes 5898244
where the time goes:
time: 98.3 us; the launch traced here: 97.7 us
  matrix products  27.7 us (28%)
  other arithmetic  20.9 us (21%)
  starting transfers between devices  13.4 us (14%)
  local copies, waits for them, and re-layouts  11.9 us (12%)
  blocking collectives  10.7 us (11%)
  waiting for transfers between devices  10.2 us (10%)
  between operations  3 us (3%)
    all_to_all x1, blocking collectives, local(): lax.all_to_all(back, 'wave', split_axis=3, concat_axis=0, tiled=True)  10.7 us
    dot_general x1, matrix products, local(): lax.dot_general(masked, spec, (((2,), (2,)), ((0,), (0,))), preferred_ele...  8.57 us
    dot_general x1, matrix products, local(): lax.dot_general(returned, masked, (((2,), (1,)), ((0,), (0,))), preferred...  8.31 us
    cos x2, other arithmetic, trig(): return (jnp.cos(angles), jnp.sin(angles))  7.33 us
    all_to_all x1, starting transfers between devices, local(): lax.all_to_all(coefficients, 'wave', split_axis=0, concat_axis=3, tiled=T...  6.35 us
    all_to_all x1, waiting for transfers between devices, local(): lax.all_to_all(product, 'tile', split_axis=0, concat_axis=1, tiled=True)  5.11 us
    select_n x1, other arithmetic, local(): jnp.where(upper, zero, legendre)  5.11 us
    all_to_all x1, waiting for transfers between devices, local(): lax.all_to_all(grid_values, 'tile', split_axis=1, concat_axis=0, tiled=True)  5.08 us
  transfers between devices with their start and end apart: 3, of which 2 were waited for; matrix products, arithmetic and copies ran while one was open for 18% of the time, Pallas kernels for 0%

commit v1 on v0

--- a/solution.py
+++ b/solution.py
@@ -157,7 +157,29 @@
         back, hot, (((2,), (2,)), ((0,), (0,))), preferred_element_type=F32
     ).astype(BF16)
     back = back.reshape(2, 2, 2 * cols, PAIRS).transpose(1, 0, 2, 3)
-    returned = lax.all_to_all(back, "wave", split_axis=3, concat_axis=0, tiled=True)
+
+    def lift_the_trees(raw, array_dim, which_dim):
+        tile_out, v_now = (jax.lax.axis_size("wave"), jax.lax.axis_index("wave"))
+        g_now = raw.shape[array_dim] // tile_out
+        w_next = list(raw.shape)
+        w_next[array_dim] = g_now
+        mixed_arr = w_next[which_dim]
+        w_next[which_dim] = mixed_arr * tile_out
+        long_array = jnp.zeros(w_next, raw.dtype)
+        j = 0
+        while j < tile_out:
+            arr_now = lax.dynamic_slice_in_dim(raw, (v_now ^ j) * g_now, g_now, axis=array_dim)
+            if j:
+                arr_now = jax.lax.ppermute(
+                    arr_now, axis_name="wave", perm=[(i, i ^ j) for i in range(tile_out)]
+                )
+            long_array = lax.dynamic_update_slice_in_dim(
+                long_array, arr_now, (v_now ^ j) * mixed_arr, axis=which_dim
+            )
+            j += 1
+        return long_array
+
+    returned = lift_the_trees(back, 3, 0)
     returned = returned.transpose(3, 2, 1, 0).reshape(slots, 2 * cols, 2 * lat_count)
     result = lax.dot_general(
         returned, masked, (((2,), (1,)), ((0,), (0,))), preferred_element_type=F32

time: 98.3 us -> 95.2 us (0.968)
  blocking collectives: 10.7 us -> 0 us
  waiting for transfers between devices: 10.2 us -> 15.6 us
  starting transfers between devices: 13.4 us -> 18.2 us
  local copies, waits for them, and re-layouts: 11.9 us -> 8.84 us
    all_to_all x1 -> x0, blocking collectives: 10.7 us -> none  [local(): lax.all_to_all(back, 'wave', split_axis=3, concat_axis=0, tiled=True)]
    ppermute x0 -> x3, waiting for transfers between devices: none -> 5.44 us  [lift_the_trees(): jax.lax.ppermute(arr_now, axis_name='wave', perm=[(i, i ^ j) for i in ran...]
    ppermute x0 -> x3, starting transfers between devices: none -> 4.53 us  [lift_the_trees(): jax.lax.ppermute(arr_now, axis_name='wave', perm=[(i, i ^ j) for i in ran...]
    unnamed x12, local copies, waits for them, and re-layouts: 1.62 us -> 0.1 us
  transfers between devices with their start and end apart: 3 -> 6, of which waited for: 2 -> 4; matrix products, arithmetic and copies ran while one was open for 18% -> 19% of each run, Pallas kernels for 0% -> 0%
where the time goes in v1:
time: 95.2 us; the launch traced here: 94.6 us
  matrix products  27.7 us (29%)
  other arithmetic  21 us (22%)
  starting transfers between devices  18.2 us (19%)
  waiting for transfers between devices  15.6 us (16%)
  local copies, waits for them, and re-layouts  8.84 us (9%)
  between operations  3.33 us (3%)
    dot_general x1, matrix products, local(): lax.dot_general(masked, spec, (((2,), (2,)), ((0,), (0,))), preferred_ele...  8.57 us
    dot_general x1, matrix products, local(): lax.dot_general(returned, masked, (((2,), (1,)), ((0,), (0,))), preferred...  8.31 us
    cos x2, other arithmetic, trig(): return (jnp.cos(angles), jnp.sin(angles))  7.33 us
    all_to_all x1, starting transfers between devices, local(): lax.all_to_all(coefficients, 'wave', split_axis=0, concat_axis=3, tiled=T...  6.35 us
    ppermute x3, waiting for transfers between devices, lift_the_trees(): jax.lax.ppermute(arr_now, axis_name='wave', perm=[(i, i ^ j) for i in ran...  5.44 us
    all_to_all x1, waiting for transfers between devices, local(): lax.all_to_all(product, 'tile', split_axis=0, concat_axis=1, tiled=True)  5.11 us
    select_n x1, other arithmetic, local(): jnp.where(upper, zero, legendre)  5.11 us
    all_to_all x1, waiting for transfers between devices, local(): lax.all_to_all(grid_values, 'tile', split_axis=1, concat_axis=0, tiled=True)  5.08 us
  transfers between devices with their start and end apart: 6, of which 4 were waited for; matrix products, arithmetic and copies ran while one was open for 19% of the time, Pallas kernels for 0%

profile of v1, /device:TPU:0, one launch (start us, length us, event | category | flops | bytes accessed | tf_op | source)
XLA Modules:
  0.0 94.6 jit_solution(5233901499985150996)
XLA Ops:
  0.0 0.8 dynamic-slice_subtract_fusion
  1.0 5.1 %broadcast_select_fusion.1 = (bf16[160,8,1281]{2,1,0:T(8,128)(2,1)}, bf16[160,8,1281]{2,1,0:T(8,128)(2,1)}) fusion(bf16[160,8,1281]{2,1,0:T(8,128)(2,1)} %param.4, pred[160,1281]{1,0:T(8,128)(4,1)S(1)} %iota_compare_fusion), kind=kLoop, calls=%fused_computation.10 | loop fusion | flops 3279360 | bytes 10043040 | tf_op jit(solution)/shard_map/jit(_where)/select_n | solution.py:72
  6.1 8.6 %fusion.12 = bf16[160,2,8,16]{3,2,1,0:T(8,128)(2,1)S(1)} fusion(bf16[160,2,8,1281]{3,2,1,0:T(8,128)(2,1)} %param.3, bf16[160,8,1281]{2,1,0:T(8,128)(2,1)} %get-tuple-element.27, bf16[160,8,1281]{2,1,0:T(8,128)(2,1)} %get-tuple-element.26), kind=kOutput, calls=%fused_computation.19 | convolution fusion | flops 118097920 | bytes 13199360 | tf_op jit(solution)/shard_map/dot_general | solution.py:96
  14.6 1.2 %copy.51 = bf16[160,2,8,16]{0,3,1,2:T(8,128)(2,1)} copy(bf16[160,2,8,16]{3,2,1,0:T(8,128)(2,1)S(1)} %fusion.12) | data formatting | bytes 163840 | tf_op jit(solution)/shard_map/reshape | solution.py:98
  15.9 6.3 %all-to-all-start = ((bf16[8,2,16,160]{3,2,1,0:T(8,128)(2,1)}), bf16[8,2,16,160]{3,2,1,0:T(8,128)(2,1)S(1)}, u32[]{:S(2)}, u32[]{:S(2)}) async-start(bf16[8,2,16,160]{3,2,1,0:T(8,128)(2,1)} %bitcast.5), calls=%async_computation | async-start | bytes 262144 | tf_op jit(solution)/shard_map/all_to_all | solution.py:101
  25.9 1.3 %iota_compare_fusion.2 = (pred[1536]{0:T(1024)(128)(4,1)S(1)}, pred[1536]{0:T(1024)(128)(4,1)S(1)}) fusion(s32[]{:T(128)S(6)} %select_n.254, s32[]{:T(128)} %bitcast.2, s32[]{:T(128)} %bitcast.13), kind=kLoop, calls=%fused_computation.140 | loop fusion | flops 7680 | bytes 3084 | tf_op jit(solution)/shard_map/ge | solution.py:84
  27.3 1.3 %compare_select_fusion.1 = (s32[1536]{0:T(1024)S(1)}, f32[1536]{0:T(1024)S(1)}) fusion(s32[]{:T(128)} %bitcast.2, s32[]{:T(128)} %bitcast.13, s32[]{:T(128)S(6)} %select_n.254), kind=kLoop, calls=%fused_computation.127 | loop fusion | flops 7680 | bytes 12300 | tf_op jit(solution)/shard_map/jit(remainder)/jit(_where)/select_n | solution.py:30
  28.7 2.1 %fusion.39 = (f32[20,1536]{1,0:T(8,128)S(1)}, f32[20,1536]{1,0:T(8,128)S(1)}) fusion(f32[1536]{0:T(1024)S(1)} %get-tuple-element.82, pred[1536]{0:T(1024)(128)(4,1)S(1)} %get-tuple-element.84, s32[1536]{0:T(1024)S(1)} %get-tuple-element.81, s32[1536]{0:T(1024)S(1)} %subtract_select_fusion, s32[20]{0:T(128)S(1)} %iota_multiply_fusion), kind=kLoop, calls=%fused_computation.64 | loop fusion | flops 337920 | bytes 265808 | tf_op jit(solution)/shard_map/cos | solution.py:32
  30.8 5.3 %fusion.27 = (f32[2,32,1536]{2,1,0:T(8,128)S(1)}, f32[2,32,1536]{2,1,0:T(8,128)S(1)}) fusion(f32[1536]{0:T(1024)S(1)} %get-tuple-element.82, pred[1536]{0:T(1024)(128)(4,1)S(1)} %get-tuple-element.84, s32[1536]{0:T(1024)S(1)} %get-tuple-element.81, s32[1536]{0:T(1024)S(1)} %subtract_select_fusion, s32[2,32]{1,0:T(2,128)S(1)} %multiply_add_fusion.1), kind=kLoop, calls=%fused_computation.40 | loop fusion | flops 1081344 | bytes 806656 | tf_op jit(solution)/shard_map/cos | solution.py:32
  36.1 2.5 %add_convert_fusion = (bf16[2,20,32,1536]{3,2,1,0:T(8,128)(2,1)S(1)}, bf16[2,20,32,1536]{3,2,1,0:T(8,128)(2,1)S(1)}) fusion(f32[2,32,1536]{2,1,0:T(8,128)S(1)} %get-tuple-element.66, f32[20,1536]{1,0:T(8,128)S(1)} %get-tuple-element.68, f32[2,32,1536]{2,1,0:T(8,128)S(1)} %get-tuple-element.65, f32[20,1536]{1,0:T(8,128)S(1)} %get-tuple-element.67), kind=kLoop, calls=%fused_computation | loop fusion | flops 15728640 | bytes 8896512 | tf_op jit(solution)/shard_map/convert_element_type | solution.py:44
  38.6 1.5 %fusion.76 = (bf16[1,20,32,1536]{3,2,1,0:T(8,128)(2,1)}, bf16[1,20,32,1536]{3,2,1,0:T(8,128)(2,1)S(1)}) fusion(bf16[2,20,32,1536]{3,2,1,0:T(8,128)(2,1)S(1)} %get-tuple-element.28), kind=kLoop, calls=%fused_computation.189 | loop fusion | bytes 7864320 | tf_op jit(solution)/shard_map/slice | solution.py:117
  40.1 2.3 %fusion.77 = (bf16[1,20,32,1536]{3,2,1,0:T(8,128)(2,1)}, bf16[1,20,32,1536]{3,2,1,0:T(8,128)(2,1)}) fusion(bf16[2,20,32,1536]{3,2,1,0:T(8,128)(2,1)S(1)} %get-tuple-element.29), kind=kLoop, calls=%fused_computation.190 | loop fusion | bytes 7864320 | tf_op jit(solution)/shard_map/slice | solution.py:117
  44.5 2.1 %fusion.43 = f32[32,1536]{1,0:T(8,128)S(1)} fusion(bf16[640,1536]{1,0:T(8,128)(2,1)} %bitcast.177, bf16[16,640]{1,0:T(8,128)(2,1)S(1)} %get-tuple-element.43, bf16[16,640]{1,0:T(8,128)(2,1)S(1)} %get-tuple-element.49), kind=kOutput, calls=%fused_computation.91 | convolution fusion | flops 62996480 | bytes 2203648 | tf_op jit(solution)/shard_map/dot_general | solution.py:117
  46.6 2.0 %fusion.50 = f32[32,1536]{1,0:T(8,128)S(1)} fusion(bf16[640,1536]{1,0:T(8,128)(2,1)} %bitcast.173, bf16[16,640]{1,0:T(8,128)(2,1)S(1)} %get-tuple-element.47, bf16[16,640]{1,0:T(8,128)(2,1)S(1)} %get-tuple-element.50), kind=kOutput, calls=%fused_computation.98 | convolution fusion | flops 62996480 | bytes 2203648 | tf_op jit(solution)/shard_map/dot_general | solution.py:118
  50.2 3.9 %all-to-all-start.1 = ((bf16[8,8,768]{2,0,1:T(8,128)(2,1)}), bf16[8,8,768]{2,0,1:T(8,128)(2,1)S(1)}, u32[]{:S(2)}, u32[]{:S(2)}) async-start(bf16[8,8,768]{2,0,1:T(8,128)(2,1)} %bitcast.31), calls=%async_computation.1 | async-start | bytes 196608 | tf_op jit(solution)/shard_map/all_to_all | solution.py:125
  54.3 5.1 %all-to-all-done.1 = bf16[8,8,768]{2,0,1:T(8,128)(2,1)S(1)} async-done(((bf16[8,8,768]{2,0,1:T(8,128)(2,1)}), bf16[8,8,768]{2,0,1:T(8,128)(2,1)S(1)}, u32[]{:S(2)}, u32[]{:S(2)}) %all-to-all-start.1) | async-done | bytes 98336 | tf_op jit(solution)/shard_map/all_to_all | solution.py:125
  60.2 3.4 %all-to-all-start.2 = ((bf16[8,8,768]{2,1,0:T(8,128)(2,1)}), bf16[8,8,768]{2,1,0:T(8,128)(2,1)S(1)}, u32[]{:S(2)}, u32[]{:S(2)}) async-start(bf16[8,8,768]{2,1,0:T(8,128)(2,1)} %bitcast.40), calls=%async_computation.2 | async-start | bytes 196608 | tf_op jit(solution)/shard_map/all_to_all | solution.py:127
  63.6 5.1 %all-to-all-done.2 = bf16[8,8,768]{2,1,0:T(8,128)(2,1)S(1)} async-done(((bf16[8,8,768]{2,1,0:T(8,128)(2,1)}), bf16[8,8,768]{2,1,0:T(8,128)(2,1)S(1)}, u32[]{:S(2)}, u32[]{:S(2)}) %all-to-all-start.2) | async-done | bytes 98336 | tf_op jit(solution)/shard_map/all_to_all | solution.py:127
  68.9 2.3 %fusion.85 = f32[32,640]{1,0:T(8,128)S(1)} fusion(bf16[32,1536]{1,0:T(8,128)(2,1)S(1)} %bitcast.181, bf16[640,1536]{1,0:T(8,128)(2,1)} %bitcast.175), kind=kOutput, calls=%fused_computation.198 | convolution fusion | flops 62914560 | bytes 2146304 | tf_op jit(solution)/shard_map/dot_general | solution.py:142
  75.6 2.1 %collective-permute-start = (bf16[2,2,16,160]{3,0,1,2:T(2,128)(2,1)S(1)}, bf16[2,2,16,160]{3,0,1,2:T(2,128)(2,1)S(1)}, u32[]{:S(2)}, u32[]{:S(2)}) collective-permute-start(bf16[2,2,16,160]{3,0,1,2:T(2,128)(2,1)S(1)} %bitcast.200), channel_id=1, source_target_pairs={{0,8},{8,0},{16,24},{24,16},{1,9},{9,1},{17,25},{25,17},{2,10},{10... | collective-permute-start | bytes 61448 | tf_op jit(solution)/shard_map/ppermute | solution.py:173
  77.7 2.4 %collective-permute-start.1 = (bf16[2,2,16,160]{3,0,1,2:T(2,128)(2,1)S(1)}, bf16[2,2,16,160]{3,0,1,2:T(2,128)(2,1)S(1)}, u32[]{:S(2)}, u32[]{:S(2)}) collective-permute-start(bf16[2,2,16,160]{3,0,1,2:T(2,128)(2,1)S(1)} %bitcast.199), channel_id=1, source_target_pairs={{0,16},{8,24},{16,0},{24,8},{1,17},{9,25},{17,1},{25,9},{2,18},{10... | collective-permute-start | bytes 61448 | tf_op jit(solution)/shard_map/ppermute | solution.py:173
  80.3 2.4 %collective-permute-done.1 = bf16[2,2,16,160]{3,0,1,2:T(2,128)(2,1)S(1)} collective-permute-done((bf16[2,2,16,160]{3,0,1,2:T(2,128)(2,1)S(1)}, bf16[2,2,16,160]{3,0,1,2:T(2,128)(2,1)S(1)}, u32[]{:S(2)}, u32[]{:S(2)}) %collective-permute-start.1) | collective-permute-done | bytes 20512 | tf_op jit(solution)/shard_map/ppermute | solution.py:173
  82.7 3.0 %collective-permute-done.2 = bf16[2,2,16,160]{3,0,1,2:T(2,128)(2,1)S(1)} collective-permute-done((bf16[2,2,16,160]{3,0,1,2:T(2,128)(2,1)S(1)}, bf16[2,2,16,160]{3,0,1,2:T(2,128)(2,1)S(1)}, u32[]{:S(2)}, u32[]{:S(2)}) %collective-permute-start.2) | collective-permute-done | bytes 20512 | tf_op jit(solution)/shard_map/ppermute | solution.py:173
  86.3 8.3 %convert_bitcast_fusion = bf16[160,2,8,1281]{3,2,1,0:T(8,128)(2,1)} fusion(bf16[160,16,16]{2,1,0:T(8,128)(2,1)S(1)} %copy.65, bf16[160,8,1281]{2,1,0:T(8,128)(2,1)} %get-tuple-element.27, bf16[160,8,1281]{2,1,0:T(8,128)(2,1)} %get-tuple-element.26), kind=kOutput, calls=%fused_computation.5 | convolution fusion | flops 121336320 | bytes 13199360 | tf_op jit(solution)/shard_map/dot_general | solution.py:184
  (96 shorter events, 10.9 us)
Async XLA Ops:
  15.9 27.0 %all-to-all-start = ((bf16[8,2,16,160]{3,2,1,0:T(8,128)(2,1)}), bf16[8,2,16,160]{3,2,1,0:T(8,128)(2,1)S(1)}, u32[]{:S(2)}, u32[]{:S(2)}) async-start(bf16[8,2,16,160]{3,2,1,0:T(8,128)(2,1)} %bitcast.5), calls=%async_computation | async-start | bytes 262144 | tf_op jit(solution)/shard_map/all_to_all | solution.py:101
  40.1 3.1 %copy-start.3 = (s32[640]{0:T(1024)S(1)}, s32[640]{0:T(1024)}, u32[]{:S(2)}) copy-start(s32[640]{0:T(1024)} %param.5) | copy-start | bytes 7684
  44.4 4.2 %copy-start.1 = (bf16[1,20,32,1536]{3,2,1,0:T(8,128)(2,1)S(1)}, bf16[1,20,32,1536]{3,2,1,0:T(8,128)(2,1)}, u32[]{:S(2)}) copy-start(bf16[1,20,32,1536]{3,2,1,0:T(8,128)(2,1)} %get-tuple-element.22) | copy-start | bytes 5898244
  50.2 9.1 %all-to-all-start.1 = ((bf16[8,8,768]{2,0,1:T(8,128)(2,1)}), bf16[8,8,768]{2,0,1:T(8,128)(2,1)S(1)}, u32[]{:S(2)}, u32[]{:S(2)}) async-start(bf16[8,8,768]{2,0,1:T(8,128)(2,1)} %bitcast.31), calls=%async_computation.1 | async-start | bytes 196608 | tf_op jit(solution)/shard_map/all_to_all | solution.py:125
  60.2 8.5 %all-to-all-start.2 = ((bf16[8,8,768]{2,1,0:T(8,128)(2,1)}), bf16[8,8,768]{2,1,0:T(8,128)(2,1)S(1)}, u32[]{:S(2)}, u32[]{:S(2)}) async-start(bf16[8,8,768]{2,1,0:T(8,128)(2,1)} %bitcast.40), calls=%async_computation.2 | async-start | bytes 196608 | tf_op jit(solution)/shard_map/all_to_all | solution.py:127
  68.7 2.5 %copy-start.2 = (bf16[1,20,32,1536]{3,2,1,0:T(8,128)(2,1)S(1)}, bf16[1,20,32,1536]{3,2,1,0:T(8,128)(2,1)}, u32[]{:S(2)}) copy-start(bf16[1,20,32,1536]{3,2,1,0:T(8,128)(2,1)} %get-tuple-element.24) | copy-start | bytes 5898244
  68.8 3.8 %copy-start = (bf16[1,20,32,1536]{3,2,1,0:T(8,128)(2,1)S(1)}, bf16[1,20,32,1536]{3,2,1,0:T(8,128)(2,1)}, u32[]{:S(2)}) copy-start(bf16[1,20,32,1536]{3,2,1,0:T(8,128)(2,1)} %get-tuple-element.25) | copy-start | bytes 5898244
  75.6 4.6 %collective-permute-start = (bf16[2,2,16,160]{3,0,1,2:T(2,128)(2,1)S(1)}, bf16[2,2,16,160]{3,0,1,2:T(2,128)(2,1)S(1)}, u32[]{:S(2)}, u32[]{:S(2)}) collective-permute-start(bf16[2,2,16,160]{3,0,1,2:T(2,128)(2,1)S(1)} %bitcast.200), channel_id=1, source_target_pairs={{0,8},{8,0},{16,24},{24,16},{1,9},{9,1},{17,25},{25,17},{2,10},{10... | collective-permute-start | bytes 61448 | tf_op jit(solution)/shard_map/ppermute | solution.py:173
  77.7 5.0 %collective-permute-start.1 = (bf16[2,2,16,160]{3,0,1,2:T(2,128)(2,1)S(1)}, bf16[2,2,16,160]{3,0,1,2:T(2,128)(2,1)S(1)}, u32[]{:S(2)}, u32[]{:S(2)}) collective-permute-start(bf16[2,2,16,160]{3,0,1,2:T(2,128)(2,1)S(1)} %bitcast.199), channel_id=1, source_target_pairs={{0,16},{8,24},{16,0},{24,8},{1,17},{9,25},{17,1},{25,9},{2,18},{10... | collective-permute-start | bytes 61448 | tf_op jit(solution)/shard_map/ppermute | solution.py:173
  80.0 5.7 %collective-permute-start.2 = (bf16[2,2,16,160]{3,0,1,2:T(2,128)(2,1)S(1)}, bf16[2,2,16,160]{3,0,1,2:T(2,128)(2,1)S(1)}, u32[]{:S(2)}, u32[]{:S(2)}) collective-permute-start(bf16[2,2,16,160]{3,0,1,2:T(2,128)(2,1)S(1)} %bitcast.198), channel_id=1, source_target_pairs={{0,24},{8,16},{16,8},{24,0},{1,25},{9,17},{17,9},{25,1},{2,26},{10... | collective-permute-start | bytes 61448 | tf_op jit(solution)/shard_map/ppermute | solution.py:173
